TPU v7x, 32 devices: a whole 2x2x4 slice. The times are simulated.
32 devices in a mesh: groups: 2 (over y), seq: 4 (over z), head: 2 (over x), sub: 2 (over core).
Axes of the slice: x: 2, y: 2, z: 4, core: 2. Of those that a mesh axis runs over, the one named last changes fastest.
Arguments:
- hidden_states: bfloat16 [8192, 8192], P(('groups', 'seq', 'sub'), 'head'), parts along dimension 0, may hold values from -42 to 42
- key_projection_weight: bfloat16 [8192, 1024], P(('seq', 'sub'), 'head'), may hold values from -0.0625 to 0.0625
- value_projection_weight: bfloat16 [8192, 1024], P(('seq', 'sub'), 'head'), may hold values from -0.0625 to 0.0625
- head_basis_matrix: float32 [8, 128, 64], P('head'), may hold values from -0.5 to 0.5
- slot_token: int32 [8192], P(('groups', 'seq', 'sub')), parts along dimension 0, may hold values from 0 to 4095, as said below
Outputs:
- compressed_keys: bfloat16 [8192, 512], P(('groups', 'seq', 'sub'), 'head'), parts along dimension 0
- value_cache: bfloat16 [8192, 1024], P(('groups', 'seq', 'sub'), 'head'), parts along dimension 0
There are 2 independent parts, one for each index of `groups`. A program takes and returns all parts, laid end to end along the dimension named above; an argument that names none is the same for every part. Nothing has to cross between parts.
Inputs may be any that keep to these rules, and one draw needn't show every extreme that they name: `slot_token`: A permutation of the 4096 token positions. Each aligned block of 512 rows holds exactly 64 positions of each aligned block of 512 positions.
All inputs are finite; a program needn't handle non-finite values.
Results may differ from a plain program's by a relative error of at most 0.0055.
Values may be sent and summed in bfloat16 or wider, within the bound.
No kernel may reach another device: no remote copies, remote signals or barrier semaphores. Data moves between devices by JAX's collectives and lax.ppermute only.
A program may use at most 64 MiB of HBM per device.

v0:
```python
import jax
import jax.numpy as jnp
from jax import lax
from jax.sharding import PartitionSpec as P

ridge_share = 0.05


def covariance_sum(decode_key_cache, heads_here, head_dim, token_total):
    per_head_keys = decode_key_cache.reshape(decode_key_cache.shape[0], heads_here, head_dim)
    local_terms = jnp.einsum(
        "thi,thj->hij", per_head_keys, per_head_keys, preferred_element_type=jnp.float32
    )
    summed = lax.psum(local_terms, ("seq", "sub"))
    return summed / token_total


def per_device(
    hidden_states, key_projection_weight, value_projection_weight, head_basis_matrix, slot_token
):
    tokens_here = hidden_states.shape[0]
    seq_count = lax.axis_size("seq")
    core_count = lax.axis_size("sub")
    device_count = seq_count * core_count
    token_total = tokens_here * device_count
    heads_here = head_basis_matrix.shape[0]
    head_dim = head_basis_matrix.shape[1]
    rank_dim = head_basis_matrix.shape[2]
    gathered = lax.all_gather(hidden_states, "head", axis=1, tiled=True)
    key_sums = jnp.dot(
        gathered,
        lax.all_gather(key_projection_weight, ("seq", "sub"), axis=0, tiled=True),
        preferred_element_type=jnp.float32,
    )
    value_sums = jnp.dot(
        gathered,
        lax.all_gather(value_projection_weight, ("seq", "sub"), axis=0, tiled=True),
        preferred_element_type=jnp.float32,
    )
    decode_key_cache = key_sums.astype(jnp.bfloat16)
    moments = covariance_sum(decode_key_cache, heads_here, head_dim, token_total)
    value_cache = value_sums.astype(jnp.bfloat16)
    trace_vals = jnp.trace(moments, axis1=1, axis2=2)
    identity = jnp.eye(head_dim, dtype=jnp.float32)
    regular = moments + (ridge_share * trace_vals / head_dim)[:, None, None] * identity
    factor = jnp.linalg.cholesky(regular)
    by_head = jnp.transpose(
        decode_key_cache.astype(jnp.float32).reshape(tokens_here, heads_here, head_dim), (1, 0, 2)
    )
    whitened = lax.linalg.triangular_solve(
        factor, by_head, left_side=False, lower=True, transpose_a=True
    )
    basis_coefficients = jnp.einsum(
        "htd,hdr->htr", whitened, head_basis_matrix, precision=lax.Precision.HIGHEST
    )
    compressed = (
        jnp.transpose(basis_coefficients, (1, 0, 2))
        .reshape(tokens_here, heads_here * rank_dim)
        .astype(jnp.bfloat16)
    )
    row_order = jnp.argsort(slot_token)
    wanted = slot_token[row_order]
    asked = lax.all_to_all(wanted, ("seq", "sub"), split_axis=0, concat_axis=0, tiled=True)
    local_rows = asked % tokens_here
    got_coeffs, got_values = (
        lax.all_to_all(
            compressed[local_rows], ("seq", "sub"), split_axis=0, concat_axis=0, tiled=True
        ),
        lax.all_to_all(
            value_cache[local_rows], ("seq", "sub"), split_axis=0, concat_axis=0, tiled=True
        ),
    )
    inverse = jnp.argsort(row_order)
    return (got_coeffs[inverse], got_values[inverse])


def solution(mesh):
    return jax.shard_map(
        per_device,
        mesh=mesh,
        in_specs=(
            P(("groups", "seq", "sub"), "head"),
            P(("seq", "sub"), "head"),
            P(("seq", "sub"), "head"),
            P("head", None, None),
            P(("groups", "seq", "sub")),
        ),
        out_specs=(P(("groups", "seq", "sub"), "head"), P(("groups", "seq", "sub"), "head")),
        check_vma=False,
    )
```

profile of v0, /device:TPU:0, one launch (start us, length us, event | category | flops | bytes accessed | tf_op | source)
XLA Modules:
  0.0 405.3 jit_solution(3034889648175689121)
XLA Ops:
  8.7 107.6 %all-gather.4.cloned.1.call-done = bf16[512,8192]{1,0:T(8,128)(2,1)} async-done(((bf16[512,4096]{1,0:T(8,128)(2,1)}), bf16[512,8192]{1,0:T(8,128)(2,1)}) %all-gather.4.cloned.1.call-update) | async-done | bytes 8388624 | tf_op jit(solution)/shard_map/all_gather | solution.py:29
  116.3 83.7 %all-gather.6.cloned.1.call-done = bf16[8192,512]{1,0:T(8,128)(2,1)} async-done(((bf16[1024,512]{1,0:T(8,128)(2,1)}), bf16[8192,512]{1,0:T(8,128)(2,1)}) %all-gather.6.cloned.1.call-update) | async-done | bytes 8388624 | tf_op jit(solution)/shard_map/all_gather | solution.py:32
  200.0 10.3 %convolution_convert_fusion.1 = bf16[512,512]{0,1:T(8,128)(2,1)S(1)} fusion(bf16[512,8192]{1,0:T(8,128)(2,1)} %all-gather.4.cloned.1.call-done, bf16[8192,512]{1,0:T(8,128)(2,1)} %all-gather.6.cloned.1.call-done), kind=kOutput, calls=%fused_computation.6 | convolution fusion | flops 4295229440 | bytes 17301504 | tf_op jit(solution)/shard_map/dot_general | solution.py:30
  210.3 1.0 fusion.6
  211.9 3.8 sort.31
  215.7 3.5 gather_fusion
  219.9 3.5 all-to-all-start
  223.4 5.2 %all-to-all-done = s32[8,64,1]{1,2,0:T(1,128)S(1)} async-done(((s32[8,64,1]{1,2,0:T(1,128)}), s32[8,64,1]{1,2,0:T(1,128)S(1)}, u32[]{:S(2)}, u32[]{:S(2)}) %all-to-all-start) | async-done | bytes 2080 | tf_op jit(solution)/shard_map/all_to_all | solution.py:63
  230.2 34.9 %all-reduce.2.cloned.1.call-done = f32[4,128,128]{2,1,0:T(8,128)} async-done(((f32[4,128,128]{2,1,0:T(8,128)}), f32[4,128,128]{2,1,0:T(8,128)}) %all-reduce.2.cloned.1.call-update) | async-done | bytes 262160 | tf_op jit(solution)/shard_map/psum | solution.py:14
  265.1 1.1 select_reduce_fusion.1
  266.1 1.0 multiply_add_fusion
  267.3 1.1 fusion.3
  268.4 46.9 %custom-call.7 = f32[4,128,128]{2,1,0:T(8,128)S(1)} custom-call(f32[4,128,128]{2,1,0:T(8,128)S(1)} %fusion.3), custom_call_target="Cholesky" | custom-call | tf_op jit(solution)/shard_map/jit(cholesky)/cholesky | solution.py:46
  315.6 39.3 %custom-call.8 = f32[4,1,128,128]{2,3,1,0:T(8,128)S(1)} custom-call(f32[4,1,128,128]{3,2,1,0:T(8,128)S(1)} %select_bitcast_fusion), custom_call_target="InvertDiagBlocksLowerTriangular" | custom-call | tf_op jit(solution)/shard_map/triangular_solve | solution.py:50
  355.5 1.3 convolution_convert_fusion.2
  356.9 2.6 gather_fusion.1
  359.5 3.6 all-to-all-start.1
  363.1 10.2 %convolution_convert_fusion = bf16[512,512]{1,0:T(8,128)(2,1)S(1)} fusion(bf16[512,8192]{1,0:T(8,128)(2,1)} %all-gather.4.cloned.1.call-done, bf16[8192,512]{1,0:T(8,128)(2,1)} %all-gather.8.cloned.1.call-done), kind=kOutput, calls=%fused_computation.5 | convolution fusion | flops 4295229440 | bytes 17301504 | tf_op jit(solution)/shard_map/dot_general | solution.py:35
  373.4 2.6 gather_fusion.3
  376.0 4.8 %all-to-all-start.2 = ((bf16[8,64,512]{2,1,0:T(8,128)(2,1)}), bf16[8,64,512]{2,1,0:T(8,128)(2,1)S(1)}, u32[]{:S(2)}, u32[]{:S(2)}) async-start(bf16[8,64,512]{2,1,0:T(8,128)(2,1)} %bitcast.11), calls=%async_computation.2 | async-start | bytes 1048576 | tf_op jit(solution)/shard_map/all_to_all | solution.py:69
  380.8 3.8 sort.32
  384.6 2.6 gather_fusion.2
  387.2 9.0 %all-to-all-done.2 = bf16[8,64,512]{2,1,0:T(8,128)(2,1)S(1)} async-done(((bf16[8,64,512]{2,1,0:T(8,128)(2,1)}), bf16[8,64,512]{2,1,0:T(8,128)(2,1)S(1)}, u32[]{:S(2)}, u32[]{:S(2)}) %all-to-all-start.2) | async-done | bytes 524320 | tf_op jit(solution)/shard_map/all_to_all | solution.py:69
  396.2 2.6 gather_fusion.4
  (37 shorter events, 5.5 us)
Async XLA Ops:
  7.2 348.3 %copy-start = (f32[4,128,64]{1,2,0:T(8,128)S(1)}, f32[4,128,64]{1,2,0:T(8,128)}, u32[]{:S(2)}) copy-start(f32[4,128,64]{1,2,0:T(8,128)} %param.8) | copy-start | bytes 393220
  7.2 109.1 %all-gather.4.cloned.1.call-start = ((), (), s32[]{:S(2)}) async-start(), calls=%async_computation.3 | async-start | bytes 12582912 | tf_op jit(solution)/shard_map/all_gather | solution.py:29
  7.9 192.1 %all-gather.6.cloned.1.call-start = ((), (), s32[]{:S(2)}) async-start(), calls=%async_computation.4 | async-start | bytes 9437184 | tf_op jit(solution)/shard_map/all_gather | solution.py:32
  8.7 203.2 %copy-start.1 = (s32[512]{0:T(512)S(1)}, s32[512]{0:T(512)}, u32[]{:S(2)}) copy-start(s32[512]{0:T(512)} %param.9) | copy-start | bytes 6148
  8.7 256.4 %all-reduce.2.cloned.1.call-start = ((), (), s32[]{:S(2)}) async-start(), calls=%async_computation.5 | async-start | bytes 524288 | tf_op jit(solution)/shard_map/psum | solution.py:14
  211.3 151.8 %all-gather.8.cloned.1.call-start = ((), (), s32[]{:S(2)}) async-start(), calls=%async_computation.6 | async-start | bytes 9437184 | tf_op jit(solution)/shard_map/all_gather | solution.py:37
  219.9 8.7 %all-to-all-start = ((s32[8,64,1]{1,2,0:T(1,128)}), s32[8,64,1]{1,2,0:T(1,128)S(1)}, u32[]{:S(2)}, u32[]{:S(2)}) async-start(s32[8,64,1]{1,2,0:T(1,128)} %bitcast.7), calls=%async_computation | async-start | bytes 8192 | tf_op jit(solution)/shard_map/all_to_all | solution.py:63
  359.5 16.6 %all-to-all-start.1 = ((bf16[8,64,256]{2,1,0:T(8,128)(2,1)}), bf16[8,64,256]{2,1,0:T(8,128)(2,1)S(1)}, u32[]{:S(2)}, u32[]{:S(2)}) async-start(bf16[8,64,256]{2,1,0:T(8,128)(2,1)} %bitcast.9), calls=%async_computation.1 | async-start | bytes 524288 | tf_op jit(solution)/shard_map/all_to_all | solution.py:66
  376.0 20.1 %all-to-all-start.2 = ((bf16[8,64,512]{2,1,0:T(8,128)(2,1)}), bf16[8,64,512]{2,1,0:T(8,128)(2,1)S(1)}, u32[]{:S(2)}, u32[]{:S(2)}) async-start(bf16[8,64,512]{2,1,0:T(8,128)(2,1)} %bitcast.11), calls=%async_computation.2 | async-start | bytes 1048576 | tf_op jit(solution)/shard_map/all_to_all | solution.py:69
Sparse Core Ops, SparseCore 0:
  9.6 106.6 all-gather.3
  117.9 82.0 all-gather.5
  211.4 53.5 all-reduce.1
  266.6 81.1 all-gather.7
where the time goes:
time: 406 us; the launch traced here: 405 us
  waiting for transfers between devices  242 us (60%)
  other arithmetic  98 us (24%)
  matrix products  23.4 us (6%)
  local copies, waits for them, and re-layouts  15.7 us (4%)
  between operations  13.9 us (3%)
  starting transfers between devices  12.1 us (3%)
    all_gather x1, waiting for transfers between devices, per_device(): gathered = lax.all_gather(hidden_states, 'head', axis=1, tiled=True)  108 us
    all_gather x1, waiting for transfers between devices, per_device(): lax.all_gather(key_projection_weight, ('seq', 'sub'), axis=0, tiled=True)  83.7 us
    another operation x4, other arithmetic, per_device(): factor = jnp.linalg.cholesky(regular)  47.1 us
    another operation x3, other arithmetic, per_device(): lax.linalg.triangular_solve(factor, by_head, left_side=False, lower=True,...  39.4 us
    psum x1, waiting for transfers between devices, covariance_sum(): summed = lax.psum(local_terms, ('seq', 'sub'))  34.9 us
    dot_general x1, matrix products, per_device(): jnp.dot(gathered, lax.all_gather(key_projection_weight, ('seq', 'sub'), a...  10.3 us
    dot_general x1, matrix products, per_device(): jnp.dot(gathered, lax.all_gather(value_projection_weight, ('seq', 'sub'),...  10.2 us
    all_to_all x1, waiting for transfers between devices, per_device(): lax.all_to_all(value_cache[local_rows], ('seq', 'sub'), split_axis=0, con...  9 us
  transfers between devices with their start and end apart: 7, of which 5 were waited for; matrix products, arithmetic and copies ran while one was open for 30% of the time, Pallas kernels for 0%

commit v1 on v0

--- a/solution.py
+++ b/solution.py
@@ -6,12 +6,17 @@
 ridge_share = 0.05
 
 
+def gather_and_add(value, name):
+    blocks = lax.all_gather(value, name)
+    return jnp.sum(blocks, axis=0)
+
+
 def covariance_sum(decode_key_cache, heads_here, head_dim, token_total):
     per_head_keys = decode_key_cache.reshape(decode_key_cache.shape[0], heads_here, head_dim)
     local_terms = jnp.einsum(
         "thi,thj->hij", per_head_keys, per_head_keys, preferred_element_type=jnp.float32
     )
-    summed = lax.psum(local_terms, ("seq", "sub"))
+    summed = gather_and_add(local_terms, ("seq", "sub"))
     return summed / token_total
 
 

time: 406 us -> 438 us (1.079)
  waiting for transfers between devices: 242 us -> 277 us
    all_gather x1, waiting for transfers between devices: 0.02 us -> 52.6 us  [per_device(): lax.all_gather(value_projection_weight, ('seq', 'sub'), axis=0, tiled=True)]
    psum x1 -> x0, waiting for transfers between devices: 34.9 us -> none  [covariance_sum(): summed = lax.psum(local_terms, ('seq', 'sub'))]
    all_gather x0 -> x1, waiting for transfers between devices: none -> 23.4 us  [gather_and_add(): blocks = lax.all_gather(value, name)]
    all_to_all x1, waiting for transfers between devices: 9 us -> 0.01 us  [per_device(): lax.all_to_all(value_cache[local_rows], ('seq', 'sub'), split_axis=0, con...]
  transfers between devices with their start and end apart: 7 -> 7, of which waited for: 5 -> 6; matrix products, arithmetic and copies ran while one was open for 30% -> 30% of each run, Pallas kernels for 0% -> 0%
where the time goes in v1:
time: 438 us
  waiting for transfers between devices  277 us (63%)
  other arithmetic  96.8 us (22%)
  matrix products  23.4 us (5%)
  local copies, waits for them, and re-layouts  15.9 us (4%)
  between operations  14 us (3%)
  starting transfers between devices  10.6 us (2%)
    all_gather x1, waiting for transfers between devices, per_device(): gathered = lax.all_gather(hidden_states, 'head', axis=1, tiled=True)  107 us
    all_gather x1, waiting for transfers between devices, per_device(): lax.all_gather(key_projection_weight, ('seq', 'sub'), axis=0, tiled=True)  83.7 us
    all_gather x1, waiting for transfers between devices, per_device(): lax.all_gather(value_projection_weight, ('seq', 'sub'), axis=0, tiled=True)  52.6 us
    another operation x4, other arithmetic, per_device(): factor = jnp.linalg.cholesky(regular)  47.1 us
    another operation x3, other arithmetic, per_device(): lax.linalg.triangular_solve(factor, by_head, left_side=False, lower=True,...  39.4 us
    all_gather x1, waiting for transfers between devices, gather_and_add(): blocks = lax.all_gather(value, name)  23.4 us
    dot_general x1, matrix products, per_device(): jnp.dot(gathered, lax.all_gather(key_projection_weight, ('seq', 'sub'), a...  10.3 us
    dot_general x1, matrix products, per_device(): jnp.dot(gathered, lax.all_gather(value_projection_weight, ('seq', 'sub'),...  10.2 us
  transfers between devices with their start and end apart: 7, of which 6 were waited for; matrix products, arithmetic and copies ran while one was open for 30% of the time, Pallas kernels for 0%

profile of v1, /device:TPU:0, one launch (start us, length us, event | category | flops | bytes accessed | tf_op | source)
XLA Modules:
  0.0 437.8 jit_solution(368886773795501532)
XLA Ops:
  8.0 0.7 all-gather.8.cloned.1.call-update
  9.5 106.8 %all-gather.6.cloned.1.call-done = bf16[512,8192]{1,0:T(8,128)(2,1)} async-done(((bf16[512,4096]{1,0:T(8,128)(2,1)}), bf16[512,8192]{1,0:T(8,128)(2,1)}) %all-gather.6.cloned.1.call-update) | async-done | bytes 8388624 | tf_op jit(solution)/shard_map/all_gather | solution.py:34
  116.3 83.7 %all-gather.8.cloned.1.call-done = bf16[8192,512]{1,0:T(8,128)(2,1)} async-done(((bf16[1024,512]{1,0:T(8,128)(2,1)}), bf16[8192,512]{1,0:T(8,128)(2,1)}) %all-gather.8.cloned.1.call-update) | async-done | bytes 8388624 | tf_op jit(solution)/shard_map/all_gather | solution.py:37
  200.0 10.3 %convolution_convert_fusion.1 = bf16[512,512]{0,1:T(8,128)(2,1)S(1)} fusion(bf16[512,8192]{1,0:T(8,128)(2,1)} %all-gather.6.cloned.1.call-done, bf16[8192,512]{1,0:T(8,128)(2,1)} %all-gather.8.cloned.1.call-done), kind=kOutput, calls=%fused_computation.6 | convolution fusion | flops 4295229440 | bytes 17301504 | tf_op jit(solution)/shard_map/dot_general | solution.py:35
  210.3 1.0 fusion.8
  211.3 3.8 sort.31
  215.1 3.5 gather_fusion
  219.3 3.3 all-to-all-start
  222.8 5.3 %all-to-all-done = s32[8,64,1]{1,2,0:T(1,128)S(1)} async-done(((s32[8,64,1]{1,2,0:T(1,128)}), s32[8,64,1]{1,2,0:T(1,128)S(1)}, u32[]{:S(2)}, u32[]{:S(2)}) %all-to-all-start) | async-done | bytes 2080 | tf_op jit(solution)/shard_map/all_to_all | solution.py:68
  229.7 52.6 %all-gather.10.cloned.1.call-done = bf16[8192,512]{1,0:T(8,128)(2,1)} async-done(((bf16[1024,512]{1,0:T(8,128)(2,1)}), bf16[8192,512]{1,0:T(8,128)(2,1)}) %all-gather.10.cloned.1.call-update) | async-done | bytes 8388624 | tf_op jit(solution)/shard_map/all_gather | solution.py:42
  282.3 10.2 %convolution_convert_fusion = bf16[512,512]{1,0:T(8,128)(2,1)S(1)} fusion(bf16[512,8192]{1,0:T(8,128)(2,1)} %all-gather.6.cloned.1.call-done, bf16[8192,512]{1,0:T(8,128)(2,1)} %all-gather.10.cloned.1.call-done), kind=kOutput, calls=%fused_computation.5 | convolution fusion | flops 4295229440 | bytes 17301504 | tf_op jit(solution)/shard_map/dot_general | solution.py:40
  292.5 2.6 gather_fusion.3
  295.2 3.7 all-to-all-start.2
  298.9 23.4 %all-gather.12.cloned.1.call-done = f32[32,128,128]{2,1,0:T(8,128)} async-done(((f32[4,128,128]{2,1,0:T(8,128)}), f32[32,128,128]{2,1,0:T(8,128)}) %all-gather.12.cloned.1.call-update) | async-done | bytes 2097168 | tf_op jit(solution)/shard_map/all_gather | solution.py:10
  322.3 1.7 reduce_sum.19
  324.5 46.9 %custom-call.7 = f32[4,128,128]{2,1,0:T(8,128)S(1)} custom-call(f32[4,128,128]{2,1,0:T(8,128)S(1)} %copy.29), custom_call_target="Cholesky" | custom-call | tf_op jit(solution)/shard_map/jit(cholesky)/cholesky | solution.py:51
  371.7 39.3 %custom-call.8 = f32[4,1,128,128]{2,3,1,0:T(8,128)S(1)} custom-call(f32[4,1,128,128]{3,2,1,0:T(8,128)S(1)} %select_bitcast_fusion), custom_call_target="InvertDiagBlocksLowerTriangular" | custom-call | tf_op jit(solution)/shard_map/triangular_solve | solution.py:55
  411.6 1.3 convolution_convert_fusion.2
  413.0 2.6 gather_fusion.1
  415.6 3.4 all-to-all-start.1
  419.0 3.8 sort.32
  422.8 2.6 gather_fusion.4
  425.4 3.2 all-to-all-done.1
  428.7 2.6 gather_fusion.2
  (40 shorter events, 5.4 us)
Async XLA Ops:
  7.2 404.5 %copy-start = (f32[4,128,64]{1,2,0:T(8,128)S(1)}, f32[4,128,64]{1,2,0:T(8,128)}, u32[]{:S(2)}) copy-start(f32[4,128,64]{1,2,0:T(8,128)} %param.8) | copy-start | bytes 393220
  7.2 109.1 %all-gather.6.cloned.1.call-start = ((), (), s32[]{:S(2)}) async-start(), calls=%async_computation.3 | async-start | bytes 12582912 | tf_op jit(solution)/shard_map/all_gather | solution.py:34
  7.9 192.1 %all-gather.8.cloned.1.call-start = ((), (), s32[]{:S(2)}) async-start(), calls=%async_computation.4 | async-start | bytes 9437184 | tf_op jit(solution)/shard_map/all_gather | solution.py:37
  8.7 273.6 %all-gather.10.cloned.1.call-start = ((), (), s32[]{:S(2)}) async-start(), calls=%async_computation.5 | async-start | bytes 9437184 | tf_op jit(solution)/shard_map/all_gather | solution.py:42
  9.4 201.9 %copy-start.1 = (s32[512]{0:T(512)S(1)}, s32[512]{0:T(512)}, u32[]{:S(2)}) copy-start(s32[512]{0:T(512)} %param.9) | copy-start | bytes 6148
  9.4 312.9 %all-gather.12.cloned.1.call-start = ((), (), s32[]{:S(2)}) async-start(), calls=%async_computation.6 | async-start | bytes 2359296 | tf_op jit(solution)/shard_map/all_gather | solution.py:10
  219.3 8.8 %all-to-all-start = ((s32[8,64,1]{1,2,0:T(1,128)}), s32[8,64,1]{1,2,0:T(1,128)S(1)}, u32[]{:S(2)}, u32[]{:S(2)}) async-start(s32[8,64,1]{1,2,0:T(1,128)} %bitcast.8), calls=%async_computation | async-start | bytes 8192 | tf_op jit(solution)/shard_map/all_to_all | solution.py:68
  295.2 120.4 %all-to-all-start.2 = ((bf16[8,64,512]{2,1,0:T(8,128)(2,1)}), bf16[8,64,512]{2,1,0:T(8,128)(2,1)S(1)}, u32[]{:S(2)}, u32[]{:S(2)}) async-start(bf16[8,64,512]{2,1,0:T(8,128)(2,1)} %bitcast.12), calls=%async_computation.2 | async-start | bytes 1048576 | tf_op jit(solution)/shard_map/all_to_all | solution.py:74
  415.6 13.1 %all-to-all-start.1 = ((bf16[8,64,256]{2,1,0:T(8,128)(2,1)}), bf16[8,64,256]{2,1,0:T(8,128)(2,1)S(1)}, u32[]{:S(2)}, u32[]{:S(2)}) async-start(bf16[8,64,256]{2,1,0:T(8,128)(2,1)} %bitcast.10), calls=%async_computation.1 | async-start | bytes 524288 | tf_op jit(solution)/shard_map/all_to_all | solution.py:71
Sparse Core Ops, SparseCore 0:
  9.6 106.6 all-gather.5
  117.9 82.0 all-gather.7
  201.6 80.6 all-gather.9
  284.3 37.9 all-gather.11
